TPU v7x, 256 devices: a whole 4x4x8 slice. The times are simulated.
256 devices in a mesh: row: 8 (over x, core), col: 32 (over z, y).
Axes of the slice: x: 4, y: 4, z: 8, core: 2. Of those that a mesh axis runs over, the one named last changes fastest.
Arguments:
- density: bfloat16 [256, 16, 128, 128], P(('row', 'col')), as said below
- cols: int32 [256, 16], replicated, may hold values from 0 to 255, as said below
Outputs:
- new_density: float32 [256, 16, 128, 128], P(('row', 'col'))
Inputs may be any that keep to these rules, and one draw needn't show every extreme that they name: Block row b is held by the device with row index (b) // 32 and col index q = (b) % 32. cols[b, 0] = b and a row's entries are distinct. For 1 <= t <= 7, cols[b, 2t - 1] is held by a device of col index q + t and cols[b, 2t] by one of col index q - t (modulo 32); cols[b, 15] by one of col index q + 16. The pattern is symmetric with mirrored slots: if j = cols[b, s] then cols[j, s'] = b, where s' = s for s = 0 and s = 15, s' = s + 1 for odd s below 15, and s' = s - 1 for even s above 0. density[b, s] is exactly the transpose of density[cols[b, s], s'], with s' the mirrored slot.
All inputs are finite; a program needn't handle non-finite values.
Results may differ from a plain program's by a relative error of at most 0.0093.
Values may be sent and summed in bfloat16 or wider, within the bound.
No kernel may reach another device: no remote copies, remote signals or barrier semaphores. Data moves between devices by JAX's collectives and lax.ppermute only.
A program may use at most 128 MiB of HBM per device.

v0:
```python
import jax
import jax.numpy as jnp
from jax import lax
from jax.sharding import PartitionSpec as P


def shifted(value, axis, by):
    length = lax.axis_size(axis)
    return lax.ppermute(value, axis, [(i, (i + by) % length) for i in range(length)])


def slot_offsets(slot_count, grid_cols):
    offsets = [0]
    for stride in range(1, (slot_count - 2) // 2 + 1):
        offsets = offsets + [stride, -stride]
    return offsets + [grid_cols // 2]


def mirror_slots(slot_count):
    order = [0]
    for stride in range(1, (slot_count - 2) // 2 + 1):
        order = order + [2 * stride, 2 * stride - 1]
    return order + [slot_count - 1]


def per_device(density, cols):
    rows_here = density.shape[0]
    slot_count = density.shape[1]
    grid_cols = lax.axis_size("col")
    my_row = lax.axis_index("row")
    my_col = lax.axis_index("col")
    offsets = slot_offsets(slot_count, grid_cols)
    mirror = jnp.array(mirror_slots(slot_count), jnp.int32)
    shift_ids = jnp.array(offsets, jnp.int32)
    local_ids = jnp.arange(rows_here, dtype=jnp.int32)
    slot_ids = jnp.arange(slot_count, dtype=jnp.int32)
    source_col = (my_col - shift_ids) % grid_cols
    tile_rows = (my_row * grid_cols + source_col)[:, None] * rows_here + local_ids[None, :]
    left_cols = cols[tile_rows]
    targets = left_cols[slot_ids[:, None], local_ids[None, :], slot_ids[:, None]]
    target_cols = cols[targets]
    matches = left_cols[..., :, None] == target_cols[..., None, :]
    present = jnp.any(matches, axis=-1)
    found_slot = jnp.sum(jnp.where(matches, slot_ids, 0), axis=-1)
    target_rank = targets // rows_here // grid_cols * rows_here + targets % rows_here
    present_mask = present[..., None, None]
    gathered = lax.all_gather(density, "col", axis=0, tiled=True)
    left_blocks = gathered[source_col[:, None] * rows_here + local_ids[None, :]]
    column_blocks = lax.all_gather(density, "row", axis=0, tiled=True)
    right_blocks = column_blocks[target_rank[:, :, None], found_slot]
    right_blocks = jnp.where(present_mask, right_blocks, jnp.zeros((), right_blocks.dtype))
    square_tile = jnp.einsum(
        "sltab,sltcb->slac", left_blocks, right_blocks, preferred_element_type=jnp.float32
    )
    square_half = square_tile.astype(jnp.bfloat16)
    square_panel = lax.all_gather(square_half[None], "row", axis=0, tiled=True)
    inner_row = left_cols // rows_here // grid_cols
    inner_local = left_cols % rows_here
    from_square = square_panel[inner_row, mirror[found_slot], inner_local]
    from_square = jnp.where(present_mask, from_square, jnp.zeros((), from_square.dtype))
    cube_tile = jnp.einsum(
        "sltab,sltbc->slac", left_blocks, from_square, preferred_element_type=jnp.float32
    )
    new_tiles = 3.0 * square_tile - 2.0 * cube_tile
    returned_pieces = []
    for position, stride in enumerate(offsets):
        if stride == 0:
            returned_pieces.append(new_tiles[position])
        else:
            returned_pieces.append(shifted(new_tiles[position], "col", -stride))
    return jnp.stack(returned_pieces, axis=1)


def solution(mesh):
    in_specs = (P(("row", "col"), None, None, None), P())
    out_specs = P(("row", "col"), None, None, None)
    return jax.shard_map(
        per_device, mesh=mesh, in_specs=in_specs, out_specs=out_specs, check_vma=False
    )
```

profile of v0, /device:TPU:48, one launch (start us, length us, event | category | flops | bytes accessed | tf_op | source)
XLA Modules:
  0.0 314.3 jit_solution(2974334684125972960)
XLA Ops:
  6.5 0.0 all-gather.7.cloned.1.call-start
  6.5 0.7 all-gather.7.cloned.1.call-update
  7.3 0.0 all-gather.5.cloned.1.call-start
  7.3 0.7 all-gather.5.cloned.1.call-update
  8.0 0.0 all-gather.9.cloned.1.call-start
  8.1 0.8 copy.11
  8.9 0.7 compare_select_fusion.6
  9.6 0.6 gather_fusion.1
  10.2 0.7 gather_fusion.2
  10.9 0.6 gather_fusion.3
  11.4 0.4 fusion.20
  11.9 0.1 broadcast_in_dim.57
  12.0 0.1 reshape.430
  12.1 0.4 compare_reduce_fusion
  12.5 33.8 %all-gather.7.cloned.1.call-done = bf16[8,16,128,128]{3,2,1,0:T(8,128)(2,1)} async-done(((bf16[1,16,128,128]{3,2,1,0:T(8,128)(2,1)}), bf16[8,16,128,128]{3,2,1,0:T(8,128)(2,1)}) %all-gather.7.cloned.1.call-update) | async-done | bytes 4194320 | tf_op jit(solution)/shard_map/all_gather | solution.py:49
  46.3 12.1 %gather_fusion.4 = bf16[256,128,128]{2,1,0:T(8,128)(2,1)} fusion(bf16[8,16,128,128]{3,2,1,0:T(8,128)(2,1)} %all-gather.7.cloned.1.call-done, s32[256]{0:T(256)S(1)} %reshape.430), kind=kCustom, calls=%fused_computation.4 | custom fusion | bytes 16779264 | tf_op jit(solution)/shard_map/gather | solution.py:50
  58.4 127.8 %all-gather.5.cloned.1.call-done = bf16[32,16,128,128]{3,2,1,0:T(8,128)(2,1)} async-done(((bf16[1,16,128,128]{3,2,1,0:T(8,128)(2,1)}), bf16[32,16,128,128]{3,2,1,0:T(8,128)(2,1)}) %all-gather.5.cloned.1.call-update) | async-done | bytes 16777232 | tf_op jit(solution)/shard_map/all_gather | solution.py:47
  186.2 10.6 %gather_fusion = bf16[16,16,128,128]{3,2,1,0:T(8,128)(2,1)} fusion(bf16[32,16,128,128]{3,2,1,0:T(8,128)(2,1)} %all-gather.5.cloned.1.call-done, s32[1024]{0:T(1024)S(1)} %pad_clamp_fusion.3), kind=kCustom, calls=%fused_computation | custom fusion | bytes 16777280 | tf_op jit(solution)/shard_map/gather | solution.py:48
  196.8 0.0 copy-start
  196.8 9.0 %fusion.38 = (bf16[16,128,128]{2,1,0:T(8,128)(2,1)}, f32[16,128,128]{2,1,0:T(8,128)S(1)}) fusion(bf16[16,16,128,128]{3,2,1,0:T(8,128)(2,1)} %gather_fusion, bf16[16,16,128,128]{3,2,1,0:T(8,128)(2,1)} %bitcast.90, pred[16,16]{1,0:T(8,128)(4,1)S(1)} %compare_reduce_fusion), kind=kOutput, calls=%fused_computation.88 | convolution fusion | flops 1078198272 | bytes 18350336 | tf_op jit(solution)/shard_map/sltab,sltcb->slac/dot_general | solution.py:52
  205.8 0.0 all-gather.9.cloned.1.call-update
  205.8 0.1 reshape.438
  205.9 0.0 copy-done
  205.9 1.9 gather_fusion.5
  207.8 0.1 gather.43
  207.9 0.1 reshape.446
  208.0 33.0 %all-gather.9.cloned.1.call-done = bf16[128,128,128]{2,1,0:T(8,128)(2,1)} async-done(((bf16[16,128,128]{2,1,0:T(8,128)(2,1)}), bf16[128,128,128]{2,1,0:T(8,128)(2,1)}) %all-gather.9.cloned.1.call-update) | async-done | bytes 4194320 | tf_op jit(solution)/shard_map/all_gather | solution.py:56
  241.0 12.2 %gather_fusion.6 = bf16[256,128,128]{2,1,0:T(8,128)(2,1)} fusion(bf16[8,16,1,128,128]{4,3,1,0,2:T(8,128)(2,1)} %bitcast.89, s32[256]{0:T(256)S(1)} %reshape.446), kind=kCustom, calls=%fused_computation.6 | custom fusion | bytes 16780288 | tf_op jit(solution)/shard_map/gather | solution.py:59
  253.2 8.2 %fusion.17 = f32[16,128,128]{2,1,0:T(8,128)S(1)} fusion(bf16[16,16,128,128]{3,2,1,0:T(8,128)(2,1)} %gather_fusion, bf16[16,16,128,128]{3,2,1,0:T(8,128)(2,1)} %bitcast.91, pred[16,16]{1,0:T(8,128)(4,1)S(1)} %compare_reduce_fusion, f32[16,128,128]{2,1,0:T(8,128)S(1)} %get-tuple-element.23), kind=kOutput, calls=%fused_computation.18 | convolution fusion | flops 1078722560 | bytes 18874624 | tf_op jit(solution)/shard_map/sltab,sltbc->slac/dot_general | solution.py:61
  261.5 0.1 fusion.37
  261.5 0.8 collective-permute-start
  262.3 1.5 collective-permute-start.1
  263.8 1.2 collective-permute-start.2
  265.0 3.2 %collective-permute-start.3 = (f32[1,128,128]{2,1,0:T(8,128)S(1)}, f32[1,128,128]{2,1,0:T(8,128)S(1)}, u32[]{:S(2)}, u32[]{:S(2)}) collective-permute-start(f32[1,128,128]{2,1,0:T(8,128)S(1)} %get-tuple-element.18), channel_id=1, source_target_pairs={{0,2},{1,3},{2,4},{3,5},{4,6},{5,7},{6,8},{7,9},{8,10},{9,11},{10,... | collective-permute-start | bytes 196616 | tf_op jit(solution)/shard_map/ppermute | solution.py:9
  268.3 3.2 %collective-permute-start.4 = (f32[1,128,128]{2,1,0:T(8,128)S(1)}, f32[1,128,128]{2,1,0:T(8,128)S(1)}, u32[]{:S(2)}, u32[]{:S(2)}) collective-permute-start(f32[1,128,128]{2,1,0:T(8,128)S(1)} %get-tuple-element.17), channel_id=1, source_target_pairs={{0,29},{1,30},{2,31},{3,0},{4,1},{5,2},{6,3},{7,4},{8,5},{9,6},{10... | collective-permute-start | bytes 196616 | tf_op jit(solution)/shard_map/ppermute | solution.py:9
  271.4 0.0 collective-permute-done
  271.4 0.0 collective-permute-start.5
  271.4 0.0 collective-permute-done.1
  271.4 5.9 %collective-permute-start.6 = (f32[1,128,128]{2,1,0:T(8,128)S(1)}, f32[1,128,128]{2,1,0:T(8,128)S(1)}, u32[]{:S(2)}, u32[]{:S(2)}) collective-permute-start(f32[1,128,128]{2,1,0:T(8,128)S(1)} %get-tuple-element.15), channel_id=1, source_target_pairs={{0,28},{1,29},{2,30},{3,31},{4,0},{5,1},{6,2},{7,3},{8,4},{9,5},{1... | collective-permute-start | bytes 196616 | tf_op jit(solution)/shard_map/ppermute | solution.py:9
  277.3 0.0 collective-permute-done.2
  277.3 0.1 collective-permute-start.7
  277.4 0.0 collective-permute-done.3
  277.4 3.4 %collective-permute-start.8 = (f32[1,128,128]{2,1,0:T(8,128)S(1)}, f32[1,128,128]{2,1,0:T(8,128)S(1)}, u32[]{:S(2)}, u32[]{:S(2)}) collective-permute-start(f32[1,128,128]{2,1,0:T(8,128)S(1)} %get-tuple-element.13), channel_id=1, source_target_pairs={{0,27},{1,28},{2,29},{3,30},{4,31},{5,0},{6,1},{7,2},{8,3},{9,4},{... | collective-permute-start | bytes 196616 | tf_op jit(solution)/shard_map/ppermute | solution.py:9
  280.9 0.0 collective-permute-done.4
  280.9 0.2 collective-permute-start.9
  281.1 0.0 collective-permute-done.5
  281.1 3.7 %collective-permute-start.10 = (f32[1,128,128]{2,1,0:T(8,128)S(1)}, f32[1,128,128]{2,1,0:T(8,128)S(1)}, u32[]{:S(2)}, u32[]{:S(2)}) collective-permute-start(f32[1,128,128]{2,1,0:T(8,128)S(1)} %get-tuple-element.11), channel_id=1, source_target_pairs={{0,26},{1,27},{2,28},{3,29},{4,30},{5,31},{6,0},{7,1},{8,2},{9,3},... | collective-permute-start | bytes 196616 | tf_op jit(solution)/shard_map/ppermute | solution.py:9
  284.8 0.0 collective-permute-done.6
  284.8 1.7 collective-permute-start.11
  286.6 0.0 collective-permute-done.7
  286.6 10.8 %collective-permute-start.12 = (f32[1,128,128]{2,1,0:T(8,128)S(1)}, f32[1,128,128]{2,1,0:T(8,128)S(1)}, u32[]{:S(2)}, u32[]{:S(2)}) collective-permute-start(f32[1,128,128]{2,1,0:T(8,128)S(1)} %get-tuple-element.9), channel_id=1, source_target_pairs={{0,25},{1,26},{2,27},{3,28},{4,29},{5,30},{6,31},{7,0},{8,1},{9,2}... | collective-permute-start | bytes 196616 | tf_op jit(solution)/shard_map/ppermute | solution.py:9
  297.4 0.0 collective-permute-done.8
  297.4 0.1 collective-permute-start.13
  297.5 0.0 collective-permute-done.9
  297.6 3.0 collective-permute-start.14
  300.5 0.0 collective-permute-done.10
  300.5 0.0 collective-permute-done.11
  300.6 0.0 collective-permute-done.12
  300.6 5.5 %collective-permute-done.13 = f32[1,128,128]{2,1,0:T(8,128)S(1)} collective-permute-done((f32[1,128,128]{2,1,0:T(8,128)S(1)}, f32[1,128,128]{2,1,0:T(8,128)S(1)}, u32[]{:S(2)}, u32[]{:S(2)}) %collective-permute-start.13) | collective-permute-done | bytes 65568 | tf_op jit(solution)/shard_map/ppermute | solution.py:9
  306.1 0.0 copy-start.1
  306.1 0.0 collective-permute-done.14
  306.1 1.0 copy-done.1
  307.1 0.6 bitcast_dynamic-update-slice_fusion
  (33 shorter events, 0.2 us)
Async XLA Ops:
  6.5 39.8 %all-gather.7.cloned.1.call-start = ((), (), s32[]{:S(2)}) async-start(), calls=%async_computation.1 | async-start | bytes 4718592 | tf_op jit(solution)/shard_map/all_gather | solution.py:49
  7.3 179.0 %all-gather.5.cloned.1.call-start = ((), (), s32[]{:S(2)}) async-start(), calls=%async_computation | async-start | bytes 17301504 | tf_op jit(solution)/shard_map/all_gather | solution.py:47
  8.0 233.0 %all-gather.9.cloned.1.call-start = ((), (), s32[]{:S(2)}) async-start(), calls=%async_computation.2 | async-start | bytes 4718592 | tf_op jit(solution)/shard_map/all_gather | solution.py:56
  196.8 9.1 %copy-start = (s32[16]{0:T(128)S(1)}, s32[16]{0:T(128)}, u32[]{:S(2)}) copy-start(s32[16]{0:T(128)} %constant.115.clone) | copy-start | bytes 196
  261.5 9.9 %collective-permute-start = (f32[1,128,128]{2,1,0:T(8,128)S(1)}, f32[1,128,128]{2,1,0:T(8,128)S(1)}, u32[]{:S(2)}, u32[]{:S(2)}) collective-permute-start(f32[1,128,128]{2,1,0:T(8,128)S(1)} %get-tuple-element.21), channel_id=1, source_target_pairs={{0,31},{1,0},{2,1},{3,2},{4,3},{5,4},{6,5},{7,6},{8,7},{9,8},{10,9... | collective-permute-start | bytes 196616 | tf_op jit(solution)/shard_map/ppermute | solution.py:9
  262.3 9.1 %collective-permute-start.1 = (f32[1,128,128]{2,1,0:T(8,128)S(1)}, f32[1,128,128]{2,1,0:T(8,128)S(1)}, u32[]{:S(2)}, u32[]{:S(2)}) collective-permute-start(f32[1,128,128]{2,1,0:T(8,128)S(1)} %get-tuple-element.20), channel_id=1, source_target_pairs={{0,1},{1,2},{2,3},{3,4},{4,5},{5,6},{6,7},{7,8},{8,9},{9,10},{10,1... | collective-permute-start | bytes 196616 | tf_op jit(solution)/shard_map/ppermute | solution.py:9
  263.8 13.5 %collective-permute-start.2 = (f32[1,128,128]{2,1,0:T(8,128)S(1)}, f32[1,128,128]{2,1,0:T(8,128)S(1)}, u32[]{:S(2)}, u32[]{:S(2)}) collective-permute-start(f32[1,128,128]{2,1,0:T(8,128)S(1)} %get-tuple-element.19), channel_id=1, source_target_pairs={{0,30},{1,31},{2,0},{3,1},{4,2},{5,3},{6,4},{7,5},{8,6},{9,7},{10,... | collective-permute-start | bytes 196616 | tf_op jit(solution)/shard_map/ppermute | solution.py:9
  265.0 12.4 %collective-permute-start.3 = (f32[1,128,128]{2,1,0:T(8,128)S(1)}, f32[1,128,128]{2,1,0:T(8,128)S(1)}, u32[]{:S(2)}, u32[]{:S(2)}) collective-permute-start(f32[1,128,128]{2,1,0:T(8,128)S(1)} %get-tuple-element.18), channel_id=1, source_target_pairs={{0,2},{1,3},{2,4},{3,5},{4,6},{5,7},{6,8},{7,9},{8,10},{9,11},{10,... | collective-permute-start | bytes 196616 | tf_op jit(solution)/shard_map/ppermute | solution.py:9
  268.3 12.6 %collective-permute-start.4 = (f32[1,128,128]{2,1,0:T(8,128)S(1)}, f32[1,128,128]{2,1,0:T(8,128)S(1)}, u32[]{:S(2)}, u32[]{:S(2)}) collective-permute-start(f32[1,128,128]{2,1,0:T(8,128)S(1)} %get-tuple-element.17), channel_id=1, source_target_pairs={{0,29},{1,30},{2,31},{3,0},{4,1},{5,2},{6,3},{7,4},{8,5},{9,6},{10... | collective-permute-start | bytes 196616 | tf_op jit(solution)/shard_map/ppermute | solution.py:9
  271.4 9.6 %collective-permute-start.5 = (f32[1,128,128]{2,1,0:T(8,128)S(1)}, f32[1,128,128]{2,1,0:T(8,128)S(1)}, u32[]{:S(2)}, u32[]{:S(2)}) collective-permute-start(f32[1,128,128]{2,1,0:T(8,128)S(1)} %get-tuple-element.16), channel_id=1, source_target_pairs={{0,3},{1,4},{2,5},{3,6},{4,7},{5,8},{6,9},{7,10},{8,11},{9,12},{10... | collective-permute-start | bytes 196616 | tf_op jit(solution)/shard_map/ppermute | solution.py:9
  271.4 13.4 %collective-permute-start.6 = (f32[1,128,128]{2,1,0:T(8,128)S(1)}, f32[1,128,128]{2,1,0:T(8,128)S(1)}, u32[]{:S(2)}, u32[]{:S(2)}) collective-permute-start(f32[1,128,128]{2,1,0:T(8,128)S(1)} %get-tuple-element.15), channel_id=1, source_target_pairs={{0,28},{1,29},{2,30},{3,31},{4,0},{5,1},{6,2},{7,3},{8,4},{9,5},{1... | collective-permute-start | bytes 196616 | tf_op jit(solution)/shard_map/ppermute | solution.py:9
  277.3 9.3 %collective-permute-start.7 = (f32[1,128,128]{2,1,0:T(8,128)S(1)}, f32[1,128,128]{2,1,0:T(8,128)S(1)}, u32[]{:S(2)}, u32[]{:S(2)}) collective-permute-start(f32[1,128,128]{2,1,0:T(8,128)S(1)} %get-tuple-element.14), channel_id=1, source_target_pairs={{0,4},{1,5},{2,6},{3,7},{4,8},{5,9},{6,10},{7,11},{8,12},{9,13},{1... | collective-permute-start | bytes 196616 | tf_op jit(solution)/shard_map/ppermute | solution.py:9
  277.4 20.0 %collective-permute-start.8 = (f32[1,128,128]{2,1,0:T(8,128)S(1)}, f32[1,128,128]{2,1,0:T(8,128)S(1)}, u32[]{:S(2)}, u32[]{:S(2)}) collective-permute-start(f32[1,128,128]{2,1,0:T(8,128)S(1)} %get-tuple-element.13), channel_id=1, source_target_pairs={{0,27},{1,28},{2,29},{3,30},{4,31},{5,0},{6,1},{7,2},{8,3},{9,4},{... | collective-permute-start | bytes 196616 | tf_op jit(solution)/shard_map/ppermute | solution.py:9
  280.9 16.7 %collective-permute-start.9 = (f32[1,128,128]{2,1,0:T(8,128)S(1)}, f32[1,128,128]{2,1,0:T(8,128)S(1)}, u32[]{:S(2)}, u32[]{:S(2)}) collective-permute-start(f32[1,128,128]{2,1,0:T(8,128)S(1)} %get-tuple-element.12), channel_id=1, source_target_pairs={{0,5},{1,6},{2,7},{3,8},{4,9},{5,10},{6,11},{7,12},{8,13},{9,14},{... | collective-permute-start | bytes 196616 | tf_op jit(solution)/shard_map/ppermute | solution.py:9
  281.1 19.5 %collective-permute-start.10 = (f32[1,128,128]{2,1,0:T(8,128)S(1)}, f32[1,128,128]{2,1,0:T(8,128)S(1)}, u32[]{:S(2)}, u32[]{:S(2)}) collective-permute-start(f32[1,128,128]{2,1,0:T(8,128)S(1)} %get-tuple-element.11), channel_id=1, source_target_pairs={{0,26},{1,27},{2,28},{3,29},{4,30},{5,31},{6,0},{7,1},{8,2},{9,3},... | collective-permute-start | bytes 196616 | tf_op jit(solution)/shard_map/ppermute | solution.py:9
  284.8 15.7 %collective-permute-start.11 = (f32[1,128,128]{2,1,0:T(8,128)S(1)}, f32[1,128,128]{2,1,0:T(8,128)S(1)}, u32[]{:S(2)}, u32[]{:S(2)}) collective-permute-start(f32[1,128,128]{2,1,0:T(8,128)S(1)} %get-tuple-element.10), channel_id=1, source_target_pairs={{0,6},{1,7},{2,8},{3,9},{4,10},{5,11},{6,12},{7,13},{8,14},{9,15},... | collective-permute-start | bytes 196616 | tf_op jit(solution)/shard_map/ppermute | solution.py:9
  286.6 14.0 %collective-permute-start.12 = (f32[1,128,128]{2,1,0:T(8,128)S(1)}, f32[1,128,128]{2,1,0:T(8,128)S(1)}, u32[]{:S(2)}, u32[]{:S(2)}) collective-permute-start(f32[1,128,128]{2,1,0:T(8,128)S(1)} %get-tuple-element.9), channel_id=1, source_target_pairs={{0,25},{1,26},{2,27},{3,28},{4,29},{5,30},{6,31},{7,0},{8,1},{9,2}... | collective-permute-start | bytes 196616 | tf_op jit(solution)/shard_map/ppermute | solution.py:9
  297.4 8.7 %collective-permute-start.13 = (f32[1,128,128]{2,1,0:T(8,128)S(1)}, f32[1,128,128]{2,1,0:T(8,128)S(1)}, u32[]{:S(2)}, u32[]{:S(2)}) collective-permute-start(f32[1,128,128]{2,1,0:T(8,128)S(1)} %get-tuple-element.8), channel_id=1, source_target_pairs={{0,7},{1,8},{2,9},{3,10},{4,11},{5,12},{6,13},{7,14},{8,15},{9,16}... | collective-permute-start | bytes 196616 | tf_op jit(solution)/shard_map/ppermute | solution.py:9
  297.6 8.6 %collective-permute-start.14 = (f32[1,128,128]{2,1,0:T(8,128)S(1)}, f32[1,128,128]{2,1,0:T(8,128)S(1)}, u32[]{:S(2)}, u32[]{:S(2)}) collective-permute-start(f32[1,128,128]{2,1,0:T(8,128)S(1)} %get-tuple-element.7), channel_id=1, source_target_pairs={{0,16},{1,17},{2,18},{3,19},{4,20},{5,21},{6,22},{7,23},{8,24},{9,... | collective-permute-start | bytes 196616 | tf_op jit(solution)/shard_map/ppermute | solution.py:9
  306.1 1.0 copy-start.1
Sparse Core Ops, SparseCore 0:
  9.2 37.0 all-gather.6
  48.9 137.2 all-gather.4
  205.9 35.0 all-gather.8
where the time goes:
time: 314 us
  waiting for transfers between devices  202 us (64%)
  local copies, waits for them, and re-layouts  41.5 us (13%)
  starting transfers between devices  38.9 us (12%)
  matrix products  17.2 us (5%)
  between operations  13.4 us (4%)
    all_gather x1, waiting for transfers between devices, per_device(): gathered = lax.all_gather(density, 'col', axis=0, tiled=True)  128 us
    ppermute x15, starting transfers between devices, shifted(): lax.ppermute(value, axis, [(i, (i + by) % length) for i in range(length)])  38.8 us
    all_gather x1, waiting for transfers between devices, per_device(): column_blocks = lax.all_gather(density, 'row', axis=0, tiled=True)  33.8 us
    all_gather x1, waiting for transfers between devices, per_device(): square_panel = lax.all_gather(square_half[None], 'row', axis=0, tiled=True)  33 us
    gather x3, local copies, waits for them, and re-layouts, per_device(): from_square = square_panel[inner_row, mirror[found_slot], inner_local]  14.2 us
    gather x1, local copies, waits for them, and re-layouts, per_device(): right_blocks = column_blocks[target_rank[:, :, None], found_slot]  12.1 us
    gather x1, local copies, waits for them, and re-layouts, per_device(): left_blocks = gathered[source_col[:, None] * rows_here + local_ids[None, :]]  10.6 us
    dot_general x1, matrix products, per_device(): jnp.einsum('sltab,sltcb->slac', left_blocks, right_blocks, preferred_elem...  8.99 us
  transfers between devices with their start and end apart: 18, of which 4 were waited for; matrix products, arithmetic and copies ran while one was open for 6% of the time, Pallas kernels for 0%

commit v1 on v0

--- a/solution.py
+++ b/solution.py
@@ -2,6 +2,11 @@
 import jax.numpy as jnp
 from jax import lax
 from jax.sharding import PartitionSpec as P
+from jax.lax import all_to_all, axis_size
+
+
+def press_shifts_all(u):
+    return jnp.concatenate(all_to_all(jnp.stack([u] * axis_size("row"), 0), "row", 0, 0), 0)
 
 
 def shifted(value, axis, by):
@@ -46,7 +51,7 @@
     present_mask = present[..., None, None]
     gathered = lax.all_gather(density, "col", axis=0, tiled=True)
     left_blocks = gathered[source_col[:, None] * rows_here + local_ids[None, :]]
-    column_blocks = lax.all_gather(density, "row", axis=0, tiled=True)
+    column_blocks = press_shifts_all(density)
     right_blocks = column_blocks[target_rank[:, :, None], found_slot]
     right_blocks = jnp.where(present_mask, right_blocks, jnp.zeros((), right_blocks.dtype))
     square_tile = jnp.einsum(

time: 314 us -> 278 us (0.89)
  waiting for transfers between devices: 202 us -> 157 us
  starting transfers between devices: 38.9 us -> 43.4 us
  local copies, waits for them, and re-layouts: 41.5 us -> 45.7 us
    all_gather x1, waiting for transfers between devices: 128 us -> 71.2 us  [per_device(): gathered = lax.all_gather(density, 'col', axis=0, tiled=True)]
    all_to_all x0 -> x1, waiting for transfers between devices: none -> 46.5 us  [press_shifts_all(): all_to_all(jnp.stack([u] * axis_size('row'), 0), 'row', 0, 0)]
    all_gather x1 -> x0, waiting for transfers between devices: 33.8 us -> none  [per_device(): column_blocks = lax.all_gather(density, 'row', axis=0, tiled=True)]
    all_to_all x0 -> x1, starting transfers between devices: none -> 4.55 us  [press_shifts_all(): all_to_all(jnp.stack([u] * axis_size('row'), 0), 'row', 0, 0)]
    another operation x0 -> x1, local copies, waits for them, and re-layouts: none -> 4.11 us  [press_shifts_all(): jnp.stack([u] * axis_size('row'), 0)]
  transfers between devices with their start and end apart: 18 -> 18, of which waited for: 4 -> 4; matrix products, arithmetic and copies ran while one was open for 6% -> 8% of each run, Pallas kernels for 0% -> 0%
where the time goes in v1:
time: 278 us
  waiting for transfers between devices  157 us (56%)
  local copies, waits for them, and re-layouts  45.7 us (16%)
  starting transfers between devices  43.4 us (16%)
  matrix products  17.2 us (6%)
  between operations  13.7 us (5%)
    all_gather x1, waiting for transfers between devices, per_device(): gathered = lax.all_gather(density, 'col', axis=0, tiled=True)  71.2 us
    all_to_all x1, waiting for transfers between devices, press_shifts_all(): all_to_all(jnp.stack([u] * axis_size('row'), 0), 'row', 0, 0)  46.5 us
    ppermute x15, starting transfers between devices, shifted(): lax.ppermute(value, axis, [(i, (i + by) % length) for i in range(length)])  38.8 us
    all_gather x1, waiting for transfers between devices, per_device(): square_panel = lax.all_gather(square_half[None], 'row', axis=0, tiled=True)  33 us
    gather x3, local copies, waits for them, and re-layouts, per_device(): from_square = square_panel[inner_row, mirror[found_slot], inner_local]  14.2 us
    gather x1, local copies, waits for them, and re-layouts, per_device(): right_blocks = column_blocks[target_rank[:, :, None], found_slot]  12.9 us
    gather x1, local copies, waits for them, and re-layouts, per_device(): left_blocks = gathered[source_col[:, None] * rows_here + local_ids[None, :]]  10.6 us
    dot_general x1, matrix products, per_device(): jnp.einsum('sltab,sltcb->slac', left_blocks, right_blocks, preferred_elem...  8.99 us
  transfers between devices with their start and end apart: 18, of which 4 were waited for; matrix products, arithmetic and copies ran while one was open for 8% of the time, Pallas kernels for 0%

profile of v1, /device:TPU:48, one launch (start us, length us, event | category | flops | bytes accessed | tf_op | source)
XLA Modules:
  0.0 278.1 jit_solution(8824874548975398144)
XLA Ops:
  6.5 0.0 copy-start.3
  6.5 0.0 copy-start.1
  6.5 0.0 all-gather.4.cloned.1.call-start
  6.5 0.7 all-gather.4.cloned.1.call-update
  7.3 4.1 %stack.59 = bf16[8,1,16,128,128]{4,3,2,1,0:T(8,128)(2,1)} broadcast(bf16[16,128,128]{2,1,0:T(8,128)(2,1)} %bitcast.94), dimensions={2,3,4} | broadcast | bytes 4718592 | tf_op jit(solution)/shard_map/stack | solution.py:9
  11.4 4.6 %all-to-all-start = ((bf16[8,1,16,128,128]{4,3,2,1,0:T(8,128)(2,1)}), bf16[8,1,16,128,128]{4,3,2,1,0:T(8,128)(2,1)}, u32[]{:S(2)}, u32[]{:S(2)}) async-start(bf16[8,1,16,128,128]{4,3,2,1,0:T(8,128)(2,1)} %stack.59), calls=%async_computation | async-start | bytes 8388608 | tf_op jit(solution)/shard_map/all_to_all | solution.py:9
  15.9 0.0 all-gather.6.cloned.1.call-start
  16.0 0.0 copy-done.1
  16.0 0.1 copy.11
  16.1 0.0 copy-done.3
  16.1 0.6 gather_fusion.1
  16.8 0.7 gather_fusion.2
  17.4 0.6 gather_fusion.3
  18.0 0.4 fusion.20
  18.5 0.1 broadcast_in_dim.57
  18.6 0.1 reshape.437
  18.7 0.4 compare_reduce_fusion
  19.1 46.5 %all-to-all-done = bf16[8,1,16,128,128]{4,3,2,1,0:T(8,128)(2,1)} async-done(((bf16[8,1,16,128,128]{4,3,2,1,0:T(8,128)(2,1)}), bf16[8,1,16,128,128]{4,3,2,1,0:T(8,128)(2,1)}, u32[]{:S(2)}, u32[]{:S(2)}) %all-to-all-start) | async-done | bytes 4194336 | tf_op jit(solution)/shard_map/all_to_all | solution.py:9
  65.6 12.9 %gather_fusion.4 = bf16[256,128,128]{2,1,0:T(8,128)(2,1)} fusion(bf16[8,16,128,128]{3,2,1,0:T(8,128)(2,1)} %bitcast.6, s32[256]{0:T(256)S(1)} %reshape.437), kind=kCustom, calls=%fused_computation.4 | custom fusion | bytes 16779264 | tf_op jit(solution)/shard_map/gather | solution.py:55
  78.5 71.2 %all-gather.4.cloned.1.call-done = bf16[32,16,128,128]{3,2,1,0:T(8,128)(2,1)} async-done(((bf16[1,16,128,128]{3,2,1,0:T(8,128)(2,1)}), bf16[32,16,128,128]{3,2,1,0:T(8,128)(2,1)}) %all-gather.4.cloned.1.call-update) | async-done | bytes 16777232 | tf_op jit(solution)/shard_map/all_gather | solution.py:52
  149.7 10.6 %gather_fusion = bf16[16,16,128,128]{3,2,1,0:T(8,128)(2,1)} fusion(bf16[32,16,128,128]{3,2,1,0:T(8,128)(2,1)} %all-gather.4.cloned.1.call-done, s32[1024]{0:T(1024)S(1)} %pad_clamp_fusion.3), kind=kCustom, calls=%fused_computation | custom fusion | bytes 16777280 | tf_op jit(solution)/shard_map/gather | solution.py:53
  160.3 9.0 %fusion.38 = (bf16[16,128,128]{2,1,0:T(8,128)(2,1)}, f32[16,128,128]{2,1,0:T(8,128)S(1)}) fusion(bf16[16,16,128,128]{3,2,1,0:T(8,128)(2,1)} %gather_fusion, bf16[16,16,128,128]{3,2,1,0:T(8,128)(2,1)} %bitcast.92, pred[16,16]{1,0:T(8,128)(4,1)S(1)} %compare_reduce_fusion), kind=kOutput, calls=%fused_computation.88 | convolution fusion | flops 1078198272 | bytes 18350336 | tf_op jit(solution)/shard_map/sltab,sltcb->slac/dot_general | solution.py:57
  169.3 0.0 all-gather.6.cloned.1.call-update
  169.3 0.1 reshape.445
  169.4 0.0 copy-done
  169.4 1.9 gather_fusion.5
  171.3 0.1 gather.43
  171.4 0.1 reshape.453
  171.5 33.0 %all-gather.6.cloned.1.call-done = bf16[128,128,128]{2,1,0:T(8,128)(2,1)} async-done(((bf16[16,128,128]{2,1,0:T(8,128)(2,1)}), bf16[128,128,128]{2,1,0:T(8,128)(2,1)}) %all-gather.6.cloned.1.call-update) | async-done | bytes 4194320 | tf_op jit(solution)/shard_map/all_gather | solution.py:61
  204.5 12.3 %gather_fusion.6 = bf16[256,128,128]{2,1,0:T(8,128)(2,1)} fusion(bf16[8,16,1,128,128]{4,3,1,0,2:T(8,128)(2,1)} %bitcast.91, s32[256]{0:T(256)S(1)} %reshape.453), kind=kCustom, calls=%fused_computation.6 | custom fusion | bytes 16780288 | tf_op jit(solution)/shard_map/gather | solution.py:64
  216.7 8.2 %fusion.17 = f32[16,128,128]{2,1,0:T(8,128)S(1)} fusion(bf16[16,16,128,128]{3,2,1,0:T(8,128)(2,1)} %gather_fusion, bf16[16,16,128,128]{3,2,1,0:T(8,128)(2,1)} %bitcast.93, pred[16,16]{1,0:T(8,128)(4,1)S(1)} %compare_reduce_fusion, f32[16,128,128]{2,1,0:T(8,128)S(1)} %get-tuple-element.23), kind=kOutput, calls=%fused_computation.18 | convolution fusion | flops 1078722560 | bytes 18874624 | tf_op jit(solution)/shard_map/sltab,sltbc->slac/dot_general | solution.py:66
  225.0 0.1 fusion.37
  225.0 0.8 collective-permute-start
  225.8 1.5 collective-permute-start.1
  227.3 1.2 collective-permute-start.2
  228.5 3.2 %collective-permute-start.3 = (f32[1,128,128]{2,1,0:T(8,128)S(1)}, f32[1,128,128]{2,1,0:T(8,128)S(1)}, u32[]{:S(2)}, u32[]{:S(2)}) collective-permute-start(f32[1,128,128]{2,1,0:T(8,128)S(1)} %get-tuple-element.18), channel_id=1, source_target_pairs={{0,2},{1,3},{2,4},{3,5},{4,6},{5,7},{6,8},{7,9},{8,10},{9,11},{10,... | collective-permute-start | bytes 196616 | tf_op jit(solution)/shard_map/ppermute | solution.py:14
  231.8 3.2 %collective-permute-start.4 = (f32[1,128,128]{2,1,0:T(8,128)S(1)}, f32[1,128,128]{2,1,0:T(8,128)S(1)}, u32[]{:S(2)}, u32[]{:S(2)}) collective-permute-start(f32[1,128,128]{2,1,0:T(8,128)S(1)} %get-tuple-element.17), channel_id=1, source_target_pairs={{0,29},{1,30},{2,31},{3,0},{4,1},{5,2},{6,3},{7,4},{8,5},{9,6},{10... | collective-permute-start | bytes 196616 | tf_op jit(solution)/shard_map/ppermute | solution.py:14
  234.9 0.0 collective-permute-done
  234.9 0.0 collective-permute-start.5
  234.9 0.0 collective-permute-done.1
  234.9 5.9 %collective-permute-start.6 = (f32[1,128,128]{2,1,0:T(8,128)S(1)}, f32[1,128,128]{2,1,0:T(8,128)S(1)}, u32[]{:S(2)}, u32[]{:S(2)}) collective-permute-start(f32[1,128,128]{2,1,0:T(8,128)S(1)} %get-tuple-element.15), channel_id=1, source_target_pairs={{0,28},{1,29},{2,30},{3,31},{4,0},{5,1},{6,2},{7,3},{8,4},{9,5},{1... | collective-permute-start | bytes 196616 | tf_op jit(solution)/shard_map/ppermute | solution.py:14
  240.8 0.0 collective-permute-done.2
  240.8 0.1 collective-permute-start.7
  240.9 0.0 collective-permute-done.3
  241.0 3.5 %collective-permute-start.8 = (f32[1,128,128]{2,1,0:T(8,128)S(1)}, f32[1,128,128]{2,1,0:T(8,128)S(1)}, u32[]{:S(2)}, u32[]{:S(2)}) collective-permute-start(f32[1,128,128]{2,1,0:T(8,128)S(1)} %get-tuple-element.13), channel_id=1, source_target_pairs={{0,27},{1,28},{2,29},{3,30},{4,31},{5,0},{6,1},{7,2},{8,3},{9,4},{... | collective-permute-start | bytes 196616 | tf_op jit(solution)/shard_map/ppermute | solution.py:14
  244.4 0.0 collective-permute-done.4
  244.4 0.1 collective-permute-start.9
  244.6 0.0 collective-permute-done.5
  244.6 3.8 %collective-permute-start.10 = (f32[1,128,128]{2,1,0:T(8,128)S(1)}, f32[1,128,128]{2,1,0:T(8,128)S(1)}, u32[]{:S(2)}, u32[]{:S(2)}) collective-permute-start(f32[1,128,128]{2,1,0:T(8,128)S(1)} %get-tuple-element.11), channel_id=1, source_target_pairs={{0,26},{1,27},{2,28},{3,29},{4,30},{5,31},{6,0},{7,1},{8,2},{9,3},... | collective-permute-start | bytes 196616 | tf_op jit(solution)/shard_map/ppermute | solution.py:14
  248.3 0.0 collective-permute-done.6
  248.3 1.7 collective-permute-start.11
  250.1 0.0 collective-permute-done.7
  250.1 10.9 %collective-permute-start.12 = (f32[1,128,128]{2,1,0:T(8,128)S(1)}, f32[1,128,128]{2,1,0:T(8,128)S(1)}, u32[]{:S(2)}, u32[]{:S(2)}) collective-permute-start(f32[1,128,128]{2,1,0:T(8,128)S(1)} %get-tuple-element.9), channel_id=1, source_target_pairs={{0,25},{1,26},{2,27},{3,28},{4,29},{5,30},{6,31},{7,0},{8,1},{9,2}... | collective-permute-start | bytes 196616 | tf_op jit(solution)/shard_map/ppermute | solution.py:14
  260.9 0.0 collective-permute-done.8
  261.0 0.1 collective-permute-start.13
  261.1 0.0 collective-permute-done.9
  261.1 3.0 %collective-permute-start.14 = (f32[1,128,128]{2,1,0:T(8,128)S(1)}, f32[1,128,128]{2,1,0:T(8,128)S(1)}, u32[]{:S(2)}, u32[]{:S(2)}) collective-permute-start(f32[1,128,128]{2,1,0:T(8,128)S(1)} %get-tuple-element.7), channel_id=1, source_target_pairs={{0,16},{1,17},{2,18},{3,19},{4,20},{5,21},{6,22},{7,23},{8,24},{9,... | collective-permute-start | bytes 196616 | tf_op jit(solution)/shard_map/ppermute | solution.py:14
  264.0 0.0 collective-permute-done.10
  264.0 0.0 collective-permute-done.11
  264.1 0.0 collective-permute-done.12
  264.1 5.5 %collective-permute-done.13 = f32[1,128,128]{2,1,0:T(8,128)S(1)} collective-permute-done((f32[1,128,128]{2,1,0:T(8,128)S(1)}, f32[1,128,128]{2,1,0:T(8,128)S(1)}, u32[]{:S(2)}, u32[]{:S(2)}) %collective-permute-start.13) | collective-permute-done | bytes 65568 | tf_op jit(solution)/shard_map/ppermute | solution.py:14
  269.6 0.0 collective-permute-done.14
  269.7 1.0 copy-done.2
  270.6 0.6 bitcast_dynamic-update-slice_fusion
  (36 shorter events, 0.2 us)
Async XLA Ops:
  6.5 9.6 %copy-start.3 = (s32[16]{0:T(128)S(1)}, s32[16]{0:T(128)}, u32[]{:S(2)}) copy-start(s32[16]{0:T(128)} %constant.118) | copy-start | bytes 196
  6.5 9.5 %copy-start.1 = (s32[256,16]{0,1:T(8,128)S(1)}, s32[256,16]{0,1:T(8,128)}, u32[]{:S(2)}) copy-start(s32[256,16]{0,1:T(8,128)} %param.5) | copy-start | bytes 49156
  6.5 143.2 %all-gather.4.cloned.1.call-start = ((), (), s32[]{:S(2)}) async-start(), calls=%async_computation.1 | async-start | bytes 17301504 | tf_op jit(solution)/shard_map/all_gather | solution.py:52
  11.4 54.2 %all-to-all-start = ((bf16[8,1,16,128,128]{4,3,2,1,0:T(8,128)(2,1)}), bf16[8,1,16,128,128]{4,3,2,1,0:T(8,128)(2,1)}, u32[]{:S(2)}, u32[]{:S(2)}) async-start(bf16[8,1,16,128,128]{4,3,2,1,0:T(8,128)(2,1)} %stack.59), calls=%async_computation | async-start | bytes 8388608 | tf_op jit(solution)/shard_map/all_to_all | solution.py:9
  15.9 188.5 %all-gather.6.cloned.1.call-start = ((), (), s32[]{:S(2)}) async-start(), calls=%async_computation.2 | async-start | bytes 4718592 | tf_op jit(solution)/shard_map/all_gather | solution.py:61
  160.3 9.1 %copy-start = (s32[16]{0:T(128)S(1)}, s32[16]{0:T(128)}, u32[]{:S(2)}) copy-start(s32[16]{0:T(128)} %constant.115.clone) | copy-start | bytes 196
  225.0 9.9 %collective-permute-start = (f32[1,128,128]{2,1,0:T(8,128)S(1)}, f32[1,128,128]{2,1,0:T(8,128)S(1)}, u32[]{:S(2)}, u32[]{:S(2)}) collective-permute-start(f32[1,128,128]{2,1,0:T(8,128)S(1)} %get-tuple-element.21), channel_id=1, source_target_pairs={{0,31},{1,0},{2,1},{3,2},{4,3},{5,4},{6,5},{7,6},{8,7},{9,8},{10,9... | collective-permute-start | bytes 196616 | tf_op jit(solution)/shard_map/ppermute | solution.py:14
  225.8 9.1 %collective-permute-start.1 = (f32[1,128,128]{2,1,0:T(8,128)S(1)}, f32[1,128,128]{2,1,0:T(8,128)S(1)}, u32[]{:S(2)}, u32[]{:S(2)}) collective-permute-start(f32[1,128,128]{2,1,0:T(8,128)S(1)} %get-tuple-element.20), channel_id=1, source_target_pairs={{0,1},{1,2},{2,3},{3,4},{4,5},{5,6},{6,7},{7,8},{8,9},{9,10},{10,1... | collective-permute-start | bytes 196616 | tf_op jit(solution)/shard_map/ppermute | solution.py:14
  227.3 13.5 %collective-permute-start.2 = (f32[1,128,128]{2,1,0:T(8,128)S(1)}, f32[1,128,128]{2,1,0:T(8,128)S(1)}, u32[]{:S(2)}, u32[]{:S(2)}) collective-permute-start(f32[1,128,128]{2,1,0:T(8,128)S(1)} %get-tuple-element.19), channel_id=1, source_target_pairs={{0,30},{1,31},{2,0},{3,1},{4,2},{5,3},{6,4},{7,5},{8,6},{9,7},{10,... | collective-permute-start | bytes 196616 | tf_op jit(solution)/shard_map/ppermute | solution.py:14
  228.5 12.4 %collective-permute-start.3 = (f32[1,128,128]{2,1,0:T(8,128)S(1)}, f32[1,128,128]{2,1,0:T(8,128)S(1)}, u32[]{:S(2)}, u32[]{:S(2)}) collective-permute-start(f32[1,128,128]{2,1,0:T(8,128)S(1)} %get-tuple-element.18), channel_id=1, source_target_pairs={{0,2},{1,3},{2,4},{3,5},{4,6},{5,7},{6,8},{7,9},{8,10},{9,11},{10,... | collective-permute-start | bytes 196616 | tf_op jit(solution)/shard_map/ppermute | solution.py:14
  231.8 12.7 %collective-permute-start.4 = (f32[1,128,128]{2,1,0:T(8,128)S(1)}, f32[1,128,128]{2,1,0:T(8,128)S(1)}, u32[]{:S(2)}, u32[]{:S(2)}) collective-permute-start(f32[1,128,128]{2,1,0:T(8,128)S(1)} %get-tuple-element.17), channel_id=1, source_target_pairs={{0,29},{1,30},{2,31},{3,0},{4,1},{5,2},{6,3},{7,4},{8,5},{9,6},{10... | collective-permute-start | bytes 196616 | tf_op jit(solution)/shard_map/ppermute | solution.py:14
  234.9 9.6 %collective-permute-start.5 = (f32[1,128,128]{2,1,0:T(8,128)S(1)}, f32[1,128,128]{2,1,0:T(8,128)S(1)}, u32[]{:S(2)}, u32[]{:S(2)}) collective-permute-start(f32[1,128,128]{2,1,0:T(8,128)S(1)} %get-tuple-element.16), channel_id=1, source_target_pairs={{0,3},{1,4},{2,5},{3,6},{4,7},{5,8},{6,9},{7,10},{8,11},{9,12},{10... | collective-permute-start | bytes 196616 | tf_op jit(solution)/shard_map/ppermute | solution.py:14
  234.9 13.4 %collective-permute-start.6 = (f32[1,128,128]{2,1,0:T(8,128)S(1)}, f32[1,128,128]{2,1,0:T(8,128)S(1)}, u32[]{:S(2)}, u32[]{:S(2)}) collective-permute-start(f32[1,128,128]{2,1,0:T(8,128)S(1)} %get-tuple-element.15), channel_id=1, source_target_pairs={{0,28},{1,29},{2,30},{3,31},{4,0},{5,1},{6,2},{7,3},{8,4},{9,5},{1... | collective-permute-start | bytes 196616 | tf_op jit(solution)/shard_map/ppermute | solution.py:14
  240.8 9.2 %collective-permute-start.7 = (f32[1,128,128]{2,1,0:T(8,128)S(1)}, f32[1,128,128]{2,1,0:T(8,128)S(1)}, u32[]{:S(2)}, u32[]{:S(2)}) collective-permute-start(f32[1,128,128]{2,1,0:T(8,128)S(1)} %get-tuple-element.14), channel_id=1, source_target_pairs={{0,4},{1,5},{2,6},{3,7},{4,8},{5,9},{6,10},{7,11},{8,12},{9,13},{1... | collective-permute-start | bytes 196616 | tf_op jit(solution)/shard_map/ppermute | solution.py:14
  241.0 20.0 %collective-permute-start.8 = (f32[1,128,128]{2,1,0:T(8,128)S(1)}, f32[1,128,128]{2,1,0:T(8,128)S(1)}, u32[]{:S(2)}, u32[]{:S(2)}) collective-permute-start(f32[1,128,128]{2,1,0:T(8,128)S(1)} %get-tuple-element.13), channel_id=1, source_target_pairs={{0,27},{1,28},{2,29},{3,30},{4,31},{5,0},{6,1},{7,2},{8,3},{9,4},{... | collective-permute-start | bytes 196616 | tf_op jit(solution)/shard_map/ppermute | solution.py:14
  244.4 16.6 %collective-permute-start.9 = (f32[1,128,128]{2,1,0:T(8,128)S(1)}, f32[1,128,128]{2,1,0:T(8,128)S(1)}, u32[]{:S(2)}, u32[]{:S(2)}) collective-permute-start(f32[1,128,128]{2,1,0:T(8,128)S(1)} %get-tuple-element.12), channel_id=1, source_target_pairs={{0,5},{1,6},{2,7},{3,8},{4,9},{5,10},{6,11},{7,12},{8,13},{9,14},{... | collective-permute-start | bytes 196616 | tf_op jit(solution)/shard_map/ppermute | solution.py:14
  244.6 19.5 %collective-permute-start.10 = (f32[1,128,128]{2,1,0:T(8,128)S(1)}, f32[1,128,128]{2,1,0:T(8,128)S(1)}, u32[]{:S(2)}, u32[]{:S(2)}) collective-permute-start(f32[1,128,128]{2,1,0:T(8,128)S(1)} %get-tuple-element.11), channel_id=1, source_target_pairs={{0,26},{1,27},{2,28},{3,29},{4,30},{5,31},{6,0},{7,1},{8,2},{9,3},... | collective-permute-start | bytes 196616 | tf_op jit(solution)/shard_map/ppermute | solution.py:14
  248.3 15.7 %collective-permute-start.11 = (f32[1,128,128]{2,1,0:T(8,128)S(1)}, f32[1,128,128]{2,1,0:T(8,128)S(1)}, u32[]{:S(2)}, u32[]{:S(2)}) collective-permute-start(f32[1,128,128]{2,1,0:T(8,128)S(1)} %get-tuple-element.10), channel_id=1, source_target_pairs={{0,6},{1,7},{2,8},{3,9},{4,10},{5,11},{6,12},{7,13},{8,14},{9,15},... | collective-permute-start | bytes 196616 | tf_op jit(solution)/shard_map/ppermute | solution.py:14
  250.1 14.0 %collective-permute-start.12 = (f32[1,128,128]{2,1,0:T(8,128)S(1)}, f32[1,128,128]{2,1,0:T(8,128)S(1)}, u32[]{:S(2)}, u32[]{:S(2)}) collective-permute-start(f32[1,128,128]{2,1,0:T(8,128)S(1)} %get-tuple-element.9), channel_id=1, source_target_pairs={{0,25},{1,26},{2,27},{3,28},{4,29},{5,30},{6,31},{7,0},{8,1},{9,2}... | collective-permute-start | bytes 196616 | tf_op jit(solution)/shard_map/ppermute | solution.py:14
  261.0 8.7 %collective-permute-start.13 = (f32[1,128,128]{2,1,0:T(8,128)S(1)}, f32[1,128,128]{2,1,0:T(8,128)S(1)}, u32[]{:S(2)}, u32[]{:S(2)}) collective-permute-start(f32[1,128,128]{2,1,0:T(8,128)S(1)} %get-tuple-element.8), channel_id=1, source_target_pairs={{0,7},{1,8},{2,9},{3,10},{4,11},{5,12},{6,13},{7,14},{8,15},{9,16}... | collective-permute-start | bytes 196616 | tf_op jit(solution)/shard_map/ppermute | solution.py:14
  261.1 8.6 %collective-permute-start.14 = (f32[1,128,128]{2,1,0:T(8,128)S(1)}, f32[1,128,128]{2,1,0:T(8,128)S(1)}, u32[]{:S(2)}, u32[]{:S(2)}) collective-permute-start(f32[1,128,128]{2,1,0:T(8,128)S(1)} %get-tuple-element.7), channel_id=1, source_target_pairs={{0,16},{1,17},{2,18},{3,19},{4,20},{5,21},{6,22},{7,23},{8,24},{9,... | collective-permute-start | bytes 196616 | tf_op jit(solution)/shard_map/ppermute | solution.py:14
  269.6 1.0 copy-start.2
Sparse Core Ops, SparseCore 0:
  9.9 139.7 all-gather.3
  169.4 35.0 all-gather.5
